TPU v7x, 512 devices: a whole 4x4x16 slice. The times are simulated.
512 devices in a mesh: fsdp: 32 (over x, z_hi, core), ctx: 16 (over y, z_lo).
Axes of the slice: x: 4, y: 4, z: 16 (z_hi: 4, z_lo: 4; z = z_hi * 4 + z_lo), core: 2. Of those that a mesh axis runs over, the one named last changes fastest.
Arguments:
- features: bfloat16 [3, 16384, 8192], P(None, 'ctx', 'fsdp'), may hold values from -6 to 6
- short_taps: float32 [3, 3, 8192], P(None, None, 'fsdp'), may hold values from -3.5 to 3.5
- decay_rates: float32 [512, 16], P('fsdp'), may hold values from 1.5258789e-05 to 0.1
- mode_gains: float32 [512, 16], P('fsdp'), may hold values from -2.5 to 2.5
- cotangent: bfloat16 [16384, 8192], P('ctx', 'fsdp'), may hold values from -6 to 6
Outputs:
- mixer_output: bfloat16 [16384, 8192], P('ctx', 'fsdp')
- feature_grads: bfloat16 [3, 16384, 8192], P(None, 'ctx', 'fsdp')
- gain_grads: float32 [512, 16], P('fsdp')
- rate_grads: float32 [512, 16], P('fsdp')
All inputs are finite; a program needn't handle non-finite values.
Results may differ from a plain program's by a relative error of at most 0.0048.
Values may be sent and summed in bfloat16 or wider, within the bound.
A program may use at most 64 MiB of HBM per device.

v0:
```python
import jax
import jax.numpy as jnp
from jax import lax
from jax.sharding import PartitionSpec as P

precise = lax.Precision.HIGHEST
threepass = lax.Precision.HIGH


def passed_along(value, axis, steps):
    count = lax.axis_size(axis)
    leading, last = (max(0, -steps), min(count, count - steps))
    return lax.ppermute(value, axis, [(source, source + steps) for source in range(leading, last)])


def diagonal_sums(gram_acc):
    group_count, block_len, width_same = gram_acc.shape
    flipped = jnp.flip(gram_acc, axis=2)
    padded = jnp.concatenate([flipped, jnp.zeros_like(flipped)], axis=2)
    flattened = padded.reshape(group_count, 2 * block_len * block_len)[
        :, : block_len * (2 * block_len - 1)
    ]
    sheared = flattened.reshape(group_count, block_len, 2 * block_len - 1)
    return jnp.sum(sheared, axis=1)[:, block_len - 1 :]


def short_conv(taps_table, row_data, tokens, rim_rows, forward):
    summed = jnp.zeros((3, tokens, row_data.shape[2]), jnp.float32)
    for offset in range(taps_table.shape[1]):
        start_row = rim_rows - offset if forward else offset
        summed = (
            summed + taps_table[:, offset, None, :] * row_data[:, start_row : start_row + tokens, :]
        )
    return summed


def per_device(features, short_taps, decay_rates, mode_gains, cotangent):
    tokens = features.shape[1]
    channels = features.shape[2]
    group_count = decay_rates.shape[0]
    order_count = decay_rates.shape[1]
    members = channels // group_count
    rim_rows = short_taps.shape[1] - 1
    block_len = 128
    block_count = tokens // block_len
    ctx_count = lax.axis_size("ctx")
    ctx_index = lax.axis_index("ctx")
    earlier_rows = passed_along(features[:, tokens - rim_rows :, :], "ctx", 1)
    extended = jnp.concatenate([earlier_rows, features], axis=1)
    shaped = short_conv(short_taps, extended, tokens, rim_rows, True)
    query_part, key_part, value_part = (shaped[0], shaped[1], shaped[2])
    product = (key_part * value_part).astype(jnp.bfloat16)
    adjoint = cotangent * query_part
    grouped_z = product.reshape(tokens, group_count, members)
    grouped_e = adjoint.reshape(tokens, group_count, members)
    mode_coefs = mode_gains * jnp.sqrt(2.0 * decay_rates)
    rate_axis = decay_rates[:, :, None]
    positions = jnp.arange(tokens, dtype=jnp.float32)[None, None, :]
    decay_from = jnp.exp(-rate_axis * positions)
    end_tables = jnp.stack([jnp.flip(decay_from, 2), -jnp.flip(positions * decay_from, 2)])
    end_states = jnp.einsum(
        "kgns,sgm->kngm", end_tables, grouped_z.astype(jnp.float32), precision=threepass
    )
    start_state = jnp.einsum("gnt,tgm->ngm", decay_from, grouped_e, precision=precise)
    local_states = jnp.stack([end_states[0], end_states[1], start_state]).reshape(
        3, order_count, channels
    )
    rate_cols = jnp.repeat(decay_rates.T, members, axis=1)
    everyone = lax.all_gather(local_states[None], "ctx", axis=0, tiled=True)
    device_ids = jnp.arange(ctx_count, dtype=jnp.int32)
    ahead_steps = (ctx_index - 1 - device_ids).astype(jnp.float32)[:, None, None]
    behind_steps = (device_ids - ctx_index - 1).astype(jnp.float32)[:, None, None]
    ahead_weight = jnp.where(
        ahead_steps >= 0, jnp.exp(-rate_cols[None] * (tokens * jnp.maximum(ahead_steps, 0.0))), 0.0
    )
    behind_weight = jnp.where(
        behind_steps >= 0,
        jnp.exp(-rate_cols[None] * (tokens * jnp.maximum(behind_steps, 0.0))),
        0.0,
    )
    prev_state = jnp.sum(ahead_weight * everyone[:, 0], axis=0)
    prev_lagged = jnp.sum(
        ahead_weight * (everyone[:, 1] - tokens * ahead_steps * everyone[:, 0]), axis=0
    )
    next_state = jnp.sum(behind_weight * everyone[:, 2], axis=0)
    lag_axis = jnp.arange(block_len, dtype=jnp.float32)[None, None, :]
    block_pow = jnp.exp(-rate_axis * lag_axis)
    block_after = block_pow * jnp.exp(-rate_axis)
    block_moments = jnp.stack([block_after, (lag_axis + 1.0) * block_after])
    coef_after = mode_coefs[:, :, None] * block_after
    block_ends = jnp.stack([jnp.flip(block_pow, 2), -jnp.flip(lag_axis * block_pow, 2)])
    coef_tail = mode_coefs[:, :, None] * jnp.flip(block_after, 2)
    block_span = jnp.exp(-decay_rates * block_len).T[:, :, None]
    filter_taps = jnp.sum(mode_coefs[:, :, None] * block_pow, axis=1)
    lag_index = (
        jnp.arange(block_len, dtype=jnp.int32)[:, None]
        - jnp.arange(block_len, dtype=jnp.int32)[None, :]
    )
    toeplitz = jnp.where(lag_index[None] >= 0, filter_taps[:, jnp.maximum(lag_index, 0)], 0.0)
    z_blocks = grouped_z.reshape(block_count, block_len, group_count, members)
    e_blocks = grouped_e.reshape(block_count, block_len, group_count, members)

    def forward_block(carried_in, inputs):
        mode_state, lagged, first_acc, lag_acc, gram_acc = carried_in
        z_block, e_block = inputs
        z_wide = z_block.astype(jnp.float32)
        inside_part = jnp.einsum("gts,sgm->tgm", toeplitz, z_wide, precision=threepass)
        carried = jnp.einsum("gnt,ngm->tgm", coef_after, mode_state, precision=precise)
        moments = jnp.einsum("kgnt,tgm->kngm", block_moments, e_block, precision=precise)
        first_acc = first_acc + jnp.sum(moments[0] * mode_state, axis=2)
        lag_acc = lag_acc + jnp.sum(moments[0] * lagged - moments[1] * mode_state, axis=2)
        gram_acc = gram_acc + jnp.einsum("tgm,sgm->gts", e_block, z_wide, precision=precise)
        fresh_part = jnp.einsum("kgns,sgm->kngm", block_ends, z_wide, precision=threepass)
        new_lagged = block_span * lagged - block_len * block_span * mode_state + fresh_part[1]
        new_state = block_span * mode_state + fresh_part[0]
        return ((new_state, new_lagged, first_acc, lag_acc, gram_acc), inside_part + carried)

    zero_state = jnp.zeros((order_count, group_count, members), jnp.float32)
    zero_pairs = jnp.zeros((order_count, group_count), jnp.float32)
    zero_gram = jnp.zeros((group_count, block_len, block_len), jnp.float32)
    final_carry, inner_blocks = lax.scan(
        forward_block,
        (zero_state, zero_state, zero_pairs, zero_pairs, zero_gram),
        (z_blocks, e_blocks),
    )
    first_acc, lag_acc, gram_acc = (final_carry[2], final_carry[3], final_carry[4])

    def backward_block(later_state, e_block):
        inside_part = jnp.einsum("gts,tgm->sgm", toeplitz, e_block, precision=precise)
        carried = jnp.einsum("gns,ngm->sgm", coef_tail, later_state, precision=precise)
        fresh_part = jnp.einsum("gnt,tgm->ngm", block_pow, e_block, precision=precise)
        return (block_span * later_state + fresh_part, inside_part + carried)

    top_state, grad_blocks = lax.scan(backward_block, zero_state, e_blocks, reverse=True)
    prev_grouped = prev_state.reshape(order_count, group_count, members)
    lagged_grouped = prev_lagged.reshape(order_count, group_count, members)
    next_grouped = next_state.reshape(order_count, group_count, members)
    device_after = decay_from * jnp.exp(-rate_axis)
    inner_sum = inner_blocks.reshape(tokens, group_count, members) + jnp.einsum(
        "gnt,ngm->tgm", mode_coefs[:, :, None] * device_after, prev_grouped, precision=precise
    )
    first_moment = jnp.exp(-decay_rates).T[:, :, None] * start_state
    second_moment = jnp.einsum(
        "gnt,tgm->ngm", (positions + 1.0) * device_after, grouped_e, precision=precise
    )
    first_acc = first_acc + jnp.sum(first_moment * prev_grouped, axis=2)
    lag_acc = lag_acc + jnp.sum(
        first_moment * lagged_grouped - second_moment * prev_grouped, axis=2
    )
    device_tail = mode_coefs[:, :, None] * jnp.flip(device_after, 2)
    product_grad = grad_blocks.reshape(tokens, group_count, members) + jnp.einsum(
        "gns,ngm->sgm", device_tail, next_grouped, precision=precise
    )
    lag_totals = diagonal_sums(gram_acc)
    first_total = first_acc.T + jnp.sum(lag_totals[:, None, :] * block_pow, axis=2)
    lag_total = lag_acc.T - jnp.sum(lag_totals[:, None, :] * lag_axis * block_pow, axis=2)
    gain_part = jnp.sqrt(2.0 * decay_rates) * first_total
    rate_part = mode_coefs * (0.5 * first_total + decay_rates * lag_total)
    inner_flat = inner_sum.reshape(tokens, channels)
    mixer_output = (query_part * inner_flat).astype(jnp.bfloat16)
    grad_flat = product_grad.reshape(tokens, channels)
    feature_adj = jnp.stack([cotangent * inner_flat, grad_flat * value_part, grad_flat * key_part])
    later_rows = passed_along(feature_adj[:, :rim_rows, :], "ctx", -1)
    appended = jnp.concatenate([feature_adj, later_rows], axis=1)
    feature_grads = short_conv(short_taps, appended, tokens, rim_rows, False).astype(jnp.bfloat16)
    filter_local = jnp.stack([gain_part, rate_part])
    entry_count = 2 * group_count * order_count * lax.axis_size("fsdp")
    summed = lax.psum(filter_local, "ctx")
    squares = lax.psum(jnp.sum(summed * summed), "fsdp")
    factor = jnp.minimum(1.0, lax.rsqrt(squares / entry_count + 1e-06))
    clipped = summed * factor
    return (mixer_output, feature_grads, clipped[0], clipped[1])


def solution(mesh):
    return jax.shard_map(
        per_device,
        mesh=mesh,
        in_specs=(
            P(None, "ctx", "fsdp"),
            P(None, None, "fsdp"),
            P("fsdp", None),
            P("fsdp", None),
            P("ctx", "fsdp"),
        ),
        out_specs=(P("ctx", "fsdp"), P(None, "ctx", "fsdp"), P("fsdp", None), P("fsdp", None)),
        check_vma=False,
    )
```

profile of v0, /device:TPU:1, one launch (start us, length us, event | category | flops | bytes accessed | tf_op | source)
XLA Modules:
  0.0 575.3 jit_solution(6784911890546579179)
XLA Ops:
  2.2 5.1 collective-permute-start
  14.9 54.5 %gather_fusion = f32[16384,16]{1,0:T(8,128)} fusion(f32[16,128]{0,1:T(8,128)S(1)} %copy.59, s32[16384]{0:T(1024)S(1)} %bitcast_clamp_fusion), kind=kCustom, calls=%fused_computation | custom fusion | bytes 2162688 | tf_op jit(solution)/shard_map/gather | solution.py:99
  69.4 5.2 copy.60
  77.4 2.6 copy.55
  80.0 3.3 rev.26
  87.9 4.8 multiply_add_fusion
  95.4 3.3 fusion.63
  105.0 41.3 %all_gather.3 = f32[16,3,16,256]{3,2,1,0:T(8,128)S(1)} all-gather(f32[1,3,16,256]{3,2,1,0:T(8,128)S(1)} %pad_maximum_fusion.5), channel_id=1, replica_groups=mesh['fsdp'=32,'ctx'=16] {'ctx'}, dimensions={0}, use_global_device_ids=true | all-gather | bytes 835584 | tf_op jit(solution)/shard_map/all_gather | solution.py:69
  154.0 132.3 %while.38 = (s32[]{:T(128)}, f32[16,16,16]{0,2,1:T(8,128)S(1)}, f32[16,16,16]{0,2,1:T(8,128)}, f32[16,16]{0,1:T(8,128)}, f32[16,16]{0,1:T(8,128)}, /*index=5*/f3...) while((s32[]{:T(128)}, f32[16,16,16]{0,2,1:T(8,128)S(1)}, ...), condition=%wide.region_4.5_spmd.clone, body=%wide.region_1.0_spmd.clone.sunk | while | flops 101380864 | bytes 5014714 | solution.py:121
  156.8 2.9 convolution_bitcast_fusion.8
  162.6 4.5 dynamic_update_slice.17
  172.0 2.9 convolution_bitcast_fusion.8
  179.4 4.5 dynamic_update_slice.17
  188.7 2.9 convolution_bitcast_fusion.8
  196.1 4.5 dynamic_update_slice.17
  205.5 2.9 convolution_bitcast_fusion.8
  212.9 4.5 dynamic_update_slice.17
  222.2 2.9 convolution_bitcast_fusion.8
  229.6 4.5 dynamic_update_slice.17
  239.0 2.9 convolution_bitcast_fusion.8
  246.3 4.5 dynamic_update_slice.17
  255.7 2.9 convolution_bitcast_fusion.8
  263.1 4.5 dynamic_update_slice.17
  272.5 2.9 convolution_bitcast_fusion.8
  279.8 4.5 dynamic_update_slice.17
  286.4 5.8 %rev.30 = f32[16,128,128]{2,1,0:T(8,128)} reverse(f32[16,128,128]{2,1,0:T(8,128)S(1)} %get-tuple-element.242), dimensions={2} | reverse | bytes 2097152 | tf_op jit(solution)/shard_map/jit(_flip)/rev | solution.py:18
  296.3 6.3 %reshape.172 = f32[16,128,255]{2,1,0:T(8,128)} reshape(f32[16,32640]{1,0:T(8,128)} %slice.116) | data formatting | bytes 4177920 | tf_op jit(solution)/shard_map/reshape | solution.py:23
  302.6 2.4 reduce_sum.112
  307.9 2.6 fusion.68
  311.3 61.1 %psum.14 = f32[2,16,16]{2,1,0:T(8,128)S(1)} all-reduce(f32[2,16,16]{2,1,0:T(8,128)S(1)} %pad_maximum_fusion.6), channel_id=1, replica_groups=mesh['fsdp'=32,'ctx'=16] {'ctx'}, use_global_device_ids=true, to_apply=%region_15.16 | all-reduce | flops 512 | bytes 4096 | tf_op jit(solution)/shard_map/psum | solution.py:168
  373.0 5.5 rev.29
  378.5 108.7 %psum.15 = f32[]{:T(128)} all-reduce(f32[]{:T(128)} %multiply_reduce_fusion.6), channel_id=1, replica_groups=mesh['fsdp'=32,'ctx'=16] {'fsdp'}, use_global_device_ids=true, to_apply=%region_17.18 | all-reduce | flops 1 | bytes 8 | tf_op jit(solution)/shard_map/psum | solution.py:169
  491.4 49.0 %while.39 = (s32[]{:T(128)}, f32[16,16,16]{0,2,1:T(8,128)S(1)}, f32[8,128,16,16]{1,0,3,2:T(8,128)}, f32[16,16,1]{0,1,2:T(8,128)S(1)}, f32[8,128,16,16]{1,3,2,0:T...) while((s32[]{:T(128)}, f32[16,16,16]{0,2,1:T(8,128)S(1)}, ...), condition=%wide.region_7.8_spmd.clone, body=%wide.region_6.7_spmd.clone.sunk | while | flops 62996484 | bytes 2277520 | solution.py:134
  492.6 4.5 dynamic_update_slice.18
  498.8 4.5 dynamic_update_slice.18
  504.9 4.5 dynamic_update_slice.18
  511.0 4.5 dynamic_update_slice.18
  517.2 4.5 dynamic_update_slice.18
  523.3 4.5 dynamic_update_slice.18
  529.4 4.5 dynamic_update_slice.18
  535.5 4.5 dynamic_update_slice.18
  540.4 2.5 reshape.168
  543.0 2.6 fusion.61
  547.3 2.4 reshape.164
  549.6 2.6 fusion.62
  558.4 9.5 %collective-permute-done.1 = f32[3,2,256]{1,2,0:T(8,128)S(1)} collective-permute-done((f32[3,2,256]{1,2,0:T(8,128)S(1)}, f32[3,2,256]{1,2,0:T(8,128)S(1)}, u32[]{:S(2)}, u32[]{:S(2)}) %collective-permute-start.1) | collective-permute-done | bytes 6176 | tf_op jit(solution)/shard_map/ppermute | solution.py:13
  569.5 3.3 fusion.54
  572.8 2.6 copy.77
  (215 shorter events, 140.8 us)
Async XLA Ops:
  2.2 85.7 %collective-permute-start = (bf16[3,2,256]{1,2,0:T(8,128)(2,1)}, bf16[3,2,256]{1,2,0:T(8,128)(2,1)}, u32[]{:S(2)}, u32[]{:S(2)}) collective-permute-start(bf16[3,2,256]{1,2,0:T(8,128)(2,1)} %copy.56), channel_id=1, source_target_pairs={{0,1},{1,2},{2,3},{3,4},{4,5},{5,6},{6,7},{7,8},{8,9},{9,10},{10,1... | collective-permute-start | bytes 9224 | tf_op jit(solution)/shard_map/ppermute | solution.py:13
  10.3 4.0 copy-start.19
  10.3 4.3 copy-start.17
  10.3 3.4 copy-start.29
  76.7 6.5 %copy-start.28 = (f32[3,1,256]{2,1,0:T(1,128)S(1)}, f32[3,1,256]{2,1,0:T(1,128)}, u32[]{:S(2)}) copy-start(f32[3,1,256]{2,1,0:T(1,128)} %get-tuple-element.483) | copy-start | bytes 9220
  77.4 7.9 %copy-start.27 = (f32[16,16]{0,1:T(8,128)S(1)}, f32[16,16]{0,1:T(8,128)}, u32[]{:S(2)}) copy-start(f32[16,16]{0,1:T(8,128)} %get-tuple-element.489) | copy-start | bytes 3076
  83.2 4.6 copy-start.25
  92.7 1.6 copy-start
  92.7 2.6 copy-start.10
  92.7 2.7 copy-start.11
  102.1 49.1 %copy-start.8 = (f32[1024,256]{0,1:T(8,128)}, f32[1024,256]{0,1:T(8,128)S(1)}, u32[]{:S(2)}) copy-start(f32[1024,256]{0,1:T(8,128)S(1)} %convert_multiply_fusion.1) | copy-start | bytes 3145732
  103.6 47.8 %copy-start.15 = (f32[16,16,16]{2,1,0:T(8,128)}, f32[16,16,16]{2,1,0:T(8,128)S(1)}, u32[]{:S(2)}) copy-start(f32[16,16,16]{2,1,0:T(8,128)S(1)} %fusion.75) | copy-start | bytes 49156
  150.9 1.0 copy-start.12
  296.3 10.9 %copy-start.14 = (f32[16,256]{0,1:T(8,128)S(1)}, f32[16,256]{0,1:T(8,128)}, u32[]{:S(2)}) copy-start(f32[16,256]{0,1:T(8,128)} %copy.70) | copy-start | bytes 49156
  296.3 10.9 %copy-start.16 = (f32[16,16,16]{2,1,0:T(8,128)S(1)}, f32[16,16,16]{2,1,0:T(8,128)}, u32[]{:S(2)}) copy-start(f32[16,16,16]{2,1,0:T(8,128)} %copy-done.15) | copy-start | bytes 49156
  296.3 11.6 %copy-start.9 = (f32[1024,256]{0,1:T(8,128)S(1)}, f32[1024,256]{0,1:T(8,128)}, u32[]{:S(2)}) copy-start(f32[1024,256]{0,1:T(8,128)} %copy-done.8) | copy-start | bytes 3145732
  491.4 51.5 %copy-start.21 = (f32[16,256]{1,0:T(8,128)S(1)}, f32[16,256]{1,0:T(8,128)}, u32[]{:S(2)}) copy-start(f32[16,256]{1,0:T(8,128)} %get-tuple-element.414) | copy-start | bytes 49156
  491.4 51.6 %copy-start.20 = (f32[16,16]{1,0:T(8,128)S(1)}, f32[16,16]{1,0:T(8,128)}, u32[]{:S(2)}) copy-start(f32[16,16]{1,0:T(8,128)} %get-tuple-element.758) | copy-start | bytes 3076
  540.4 5.2 copy-start.1
  545.6 4.0 copy-start.18
  549.6 4.6 copy-start.2
  549.6 4.6 copy-start.4
  554.3 1.0 copy-start.6
  554.3 2.5 copy-start.22
  554.3 3.1 copy-start.13
  554.3 13.6 %copy-start.3 = (f32[1,1024,256]{1,2,0:T(8,128)S(1)}, f32[1,1024,256]{1,2,0:T(8,128)}, u32[]{:S(2)}) copy-start(f32[1,1024,256]{1,2,0:T(8,128)} %get-tuple-element.471) | copy-start | bytes 3145732
  554.3 13.6 %copy-start.5 = (f32[1,1024,256]{1,2,0:T(8,128)S(1)}, f32[1,1024,256]{1,2,0:T(8,128)}, u32[]{:S(2)}) copy-start(f32[1,1024,256]{1,2,0:T(8,128)} %get-tuple-element.472) | copy-start | bytes 3145732
  555.4 12.6 %collective-permute-start.1 = (f32[3,2,256]{1,2,0:T(8,128)S(1)}, f32[3,2,256]{1,2,0:T(8,128)S(1)}, u32[]{:S(2)}, u32[]{:S(2)}) collective-permute-start(f32[3,2,256]{1,2,0:T(8,128)S(1)} %slice.113), channel_id=1, source_target_pairs={{1,0},{2,1},{3,2},{4,3},{5,4},{6,5},{7,6},{8,7},{9,8},{10,9},{11,1... | collective-permute-start | bytes 18440 | tf_op jit(solution)/shard_map/ppermute | solution.py:13
  558.4 11.0 %copy-start.7 = (f32[1,1024,256]{1,2,0:T(8,128)S(1)}, f32[1,1024,256]{1,2,0:T(8,128)}, u32[]{:S(2)}) copy-start(f32[1,1024,256]{1,2,0:T(8,128)} %copy-done.6) | copy-start | bytes 3145732
  558.4 11.0 %copy-start.23 = (f32[3,256]{1,0:T(4,128)S(1)}, f32[3,256]{1,0:T(4,128)}, u32[]{:S(2)}) copy-start(f32[3,256]{1,0:T(4,128)} %get-tuple-element.499) | copy-start | bytes 9220
  558.4 11.0 %copy-start.24 = (f32[3,256]{1,0:T(4,128)S(1)}, f32[3,256]{1,0:T(4,128)}, u32[]{:S(2)}) copy-start(f32[3,256]{1,0:T(4,128)} %get-tuple-element.500) | copy-start | bytes 9220
  558.4 11.0 %copy-start.26 = (f32[3,1,256]{2,0,1:T(4,128)S(1)}, f32[3,1,256]{2,0,1:T(4,128)}, u32[]{:S(2)}) copy-start(f32[3,1,256]{2,0,1:T(4,128)} %copy-done.25) | copy-start | bytes 9220
where the time goes:
time: 580 us; the launch traced here: 575 us
  blocking collectives  211 us (36%)
  local copies, waits for them, and re-layouts  189 us (33%)
  matrix products  99.5 us (17%)
  other arithmetic  57.1 us (10%)
  waiting for transfers between devices  9.53 us (2%)
  starting transfers between devices  6.47 us (1%)
    psum x1, blocking collectives, per_device(): squares = lax.psum(jnp.sum(summed * summed), 'fsdp')  109 us
    dynamic_update_slice x16, local copies, waits for them, and re-layouts, per_device(): lax.scan(forward_block, (zero_state, zero_state, zero_pairs, zero_pairs,...  71.3 us
    psum x1, blocking collectives, per_device(): summed = lax.psum(filter_local, 'ctx')  61.1 us
    gather x2, local copies, waits for them, and re-layouts, per_device(): filter_taps[:, jnp.maximum(lag_index, 0)]  59.7 us
    all_gather x1, blocking collectives, per_device(): everyone = lax.all_gather(local_states[None], 'ctx', axis=0, tiled=True)  41.3 us
    dot_general x8, matrix products, forward_block(): jnp.einsum('kgnt,tgm->kngm', block_moments, e_block, precision=precise)  23.1 us
    dot_general x8, matrix products, forward_block(): jnp.einsum('tgm,sgm->gts', e_block, z_wide, precision=precise)  16.3 us
    unnamed x72, local copies, waits for them, and re-layouts  15.9 us
  transfers between devices with their start and end apart: 2, of which 1 were waited for; matrix products, arithmetic and copies ran while one was open for 14% of the time, Pallas kernels for 0%

commit v1 on v0

--- a/solution.py
+++ b/solution.py
@@ -66,7 +66,9 @@
         3, order_count, channels
     )
     rate_cols = jnp.repeat(decay_rates.T, members, axis=1)
-    everyone = lax.all_gather(local_states[None], "ctx", axis=0, tiled=True)
+    everyone = jnp.concatenate(
+        lax.all_to_all(jnp.stack([local_states[None]] * lax.axis_size("ctx")), "ctx", 0, 0), axis=0
+    )
     device_ids = jnp.arange(ctx_count, dtype=jnp.int32)
     ahead_steps = (ctx_index - 1 - device_ids).astype(jnp.float32)[:, None, None]
     behind_steps = (device_ids - ctx_index - 1).astype(jnp.float32)[:, None, None]

time: 580 us -> 538 us (0.928)
  blocking collectives: 211 us -> 170 us
  starting transfers between devices: 6.47 us -> 12.7 us
    all_gather x1 -> x0, blocking collectives: 41.3 us -> none  [per_device(): everyone = lax.all_gather(local_states[None], 'ctx', axis=0, tiled=True)]
    all_to_all x0 -> x1, starting transfers between devices: none -> 6.39 us  [per_device(): lax.all_to_all(jnp.stack([local_states[None]] * lax.axis_size('ctx')), 'c...]
    unnamed x72 -> x86, local copies, waits for them, and re-layouts: 15.9 us -> 17 us
  transfers between devices with their start and end apart: 2 -> 3, of which waited for: 1 -> 1; matrix products, arithmetic and copies ran while one was open for 14% -> 55% of each run, Pallas kernels for 0% -> 0%
where the time goes in v1:
time: 538 us; the launch traced here: 534 us
  local copies, waits for them, and re-layouts  189 us (35%)
  blocking collectives  170 us (32%)
  matrix products  96.4 us (18%)
  other arithmetic  53.2 us (10%)
  starting transfers between devices  12.7 us (2%)
  waiting for transfers between devices  8.82 us (2%)
    psum x1, blocking collectives, per_device(): squares = lax.psum(jnp.sum(summed * summed), 'fsdp')  105 us
    dynamic_update_slice x16, local copies, waits for them, and re-layouts, per_device(): lax.scan(forward_block, (zero_state, zero_state, zero_pairs, zero_pairs,...  71.2 us
    psum x1, blocking collectives, per_device(): summed = lax.psum(filter_local, 'ctx')  65.8 us
    gather x2, local copies, waits for them, and re-layouts, per_device(): filter_taps[:, jnp.maximum(lag_index, 0)]  60 us
    dot_general x8, matrix products, forward_block(): jnp.einsum('kgnt,tgm->kngm', block_moments, e_block, precision=precise)  23.1 us
    unnamed x86, local copies, waits for them, and re-layouts  17 us
    dot_general x8, matrix products, forward_block(): jnp.einsum('tgm,sgm->gts', e_block, z_wide, precision=precise)  16.3 us
    dot_general x8, matrix products, forward_block(): jnp.einsum('kgns,sgm->kngm', block_ends, z_wide, precision=threepass)  13.8 us
  transfers between devices with their start and end apart: 3, of which 1 were waited for; matrix products, arithmetic and copies ran while one was open for 55% of the time, Pallas kernels for 0%

profile of v1, /device:TPU:1, one launch (start us, length us, event | category | flops | bytes accessed | tf_op | source)
XLA Modules:
  0.0 533.8 jit_solution(9603858495399764068)
XLA Ops:
  2.2 5.0 collective-permute-start
  14.9 54.8 %gather_fusion = f32[16384,16]{1,0:T(8,128)} fusion(f32[16,128]{0,1:T(8,128)S(1)} %copy.79, s32[16384]{0:T(1024)S(1)} %bitcast_clamp_fusion), kind=kCustom, calls=%fused_computation | custom fusion | bytes 2162688 | tf_op jit(solution)/shard_map/gather | solution.py:101
  69.7 5.2 copy.80
  77.6 2.6 copy.75
  80.2 5.5 %rev.26 = f32[16,16,1024]{2,1,0:T(8,128)} reverse(f32[16,16,1024]{2,1,0:T(8,128)} %get-tuple-element.523), dimensions={2} | reverse | bytes 2097152 | tf_op jit(solution)/shard_map/jit(_flip)/rev | solution.py:60
  86.4 2.0 copy.78
  92.2 3.3 rev.29
  95.6 4.9 multiply_add_fusion
  103.1 2.5 fusion.63
  112.1 6.4 %all-to-all-start = ((f32[16,1,3,16,256]{4,3,2,1,0:T(8,128)}), f32[16,1,3,16,256]{4,3,2,1,0:T(8,128)}, u32[]{:S(2)}, u32[]{:S(2)}) async-start(f32[16,1,3,16,256]{4,3,2,1,0:T(8,128)} %stack.62), calls=%async_computation | async-start | bytes 1572864 | tf_op jit(solution)/shard_map/all_to_all | solution.py:70
  121.6 132.4 %while.38 = (s32[]{:T(128)}, f32[16,16,16]{0,2,1:T(8,128)S(1)}, f32[16,16,16]{0,2,1:T(8,128)}, f32[16,16]{0,1:T(8,128)}, f32[16,16]{0,1:T(8,128)}, /*index=5*/f3...) while((s32[]{:T(128)}, f32[16,16,16]{0,2,1:T(8,128)S(1)}, ...), condition=%wide.region_4.5_spmd.clone, body=%wide.region_1.0_spmd.clone.sunk | while | flops 101380864 | bytes 5014714 | solution.py:123
  124.4 2.9 convolution_bitcast_fusion.8
  130.2 4.5 dynamic_update_slice.17
  139.6 2.9 convolution_bitcast_fusion.8
  147.0 4.5 dynamic_update_slice.17
  156.3 2.9 convolution_bitcast_fusion.8
  163.7 4.5 dynamic_update_slice.17
  168.2 2.0 convolution_add_fusion.6
  173.1 2.9 convolution_bitcast_fusion.8
  180.5 4.5 dynamic_update_slice.17
  184.9 2.0 convolution_add_fusion.6
  189.8 2.9 convolution_bitcast_fusion.8
  197.2 4.5 dynamic_update_slice.17
  206.6 2.9 convolution_bitcast_fusion.8
  214.0 4.5 dynamic_update_slice.17
  223.3 2.9 convolution_bitcast_fusion.8
  230.7 4.5 dynamic_update_slice.17
  240.1 2.9 convolution_bitcast_fusion.8
  247.5 4.5 dynamic_update_slice.17
  254.0 5.9 %rev.30 = f32[16,128,128]{2,1,0:T(8,128)} reverse(f32[16,128,128]{2,1,0:T(8,128)S(1)} %get-tuple-element.242), dimensions={2} | reverse | bytes 2097152 | tf_op jit(solution)/shard_map/jit(_flip)/rev | solution.py:18
  264.0 6.2 %reshape.179 = f32[16,128,255]{2,1,0:T(8,128)} reshape(f32[16,32640]{1,0:T(8,128)} %slice.116) | data formatting | bytes 4177920 | tf_op jit(solution)/shard_map/reshape | solution.py:23
  274.3 49.1 %while.39 = (s32[]{:T(128)}, f32[16,16,16]{0,2,1:T(8,128)S(1)}, f32[8,128,16,16]{1,0,3,2:T(8,128)}, f32[16,16,1]{0,1,2:T(8,128)S(1)}, f32[8,128,16,16]{1,3,2,0:T...) while((s32[]{:T(128)}, f32[16,16,16]{0,2,1:T(8,128)S(1)}, ...), condition=%wide.region_7.8_spmd.clone, body=%wide.region_6.7_spmd.clone.sunk | while | flops 62996484 | bytes 2277520 | solution.py:136
  275.5 4.4 dynamic_update_slice.18
  281.6 4.4 dynamic_update_slice.18
  287.8 4.4 dynamic_update_slice.18
  293.9 4.4 dynamic_update_slice.18
  300.0 4.4 dynamic_update_slice.18
  306.1 4.4 dynamic_update_slice.18
  312.2 4.4 dynamic_update_slice.18
  318.3 4.4 dynamic_update_slice.18
  328.0 2.5 fusion.68
  330.6 65.8 %psum.14 = f32[2,16,16]{2,1,0:T(8,128)S(1)} all-reduce(f32[2,16,16]{2,1,0:T(8,128)S(1)} %pad_maximum_fusion.5), channel_id=1, replica_groups=mesh['fsdp'=32,'ctx'=16] {'ctx'}, use_global_device_ids=true, to_apply=%region_15.16 | all-reduce | flops 512 | bytes 4096 | tf_op jit(solution)/shard_map/psum | solution.py:170
  397.0 2.4 reshape.170
  399.4 104.7 %psum.15 = f32[]{:T(128)} all-reduce(f32[]{:T(128)} %multiply_reduce_fusion.6), channel_id=1, replica_groups=mesh['fsdp'=32,'ctx'=16] {'fsdp'}, use_global_device_ids=true, to_apply=%region_17.18 | all-reduce | flops 1 | bytes 8 | tf_op jit(solution)/shard_map/psum | solution.py:171
  510.6 2.3 fusion.69
  517.8 8.8 %collective-permute-done.1 = f32[3,2,256]{1,2,0:T(8,128)} collective-permute-done((f32[3,2,256]{1,2,0:T(8,128)}, f32[3,2,256]{1,2,0:T(8,128)}, u32[]{:S(2)}, u32[]{:S(2)}) %collective-permute-start.1) | collective-permute-done | bytes 6176 | tf_op jit(solution)/shard_map/ppermute | solution.py:13
  527.9 3.3 fusion.54
  531.2 2.6 copy.97
  (231 shorter events, 135.9 us)
Async XLA Ops:
  2.2 93.4 %collective-permute-start = (bf16[3,2,256]{1,2,0:T(8,128)(2,1)}, bf16[3,2,256]{1,2,0:T(8,128)(2,1)}, u32[]{:S(2)}, u32[]{:S(2)}) collective-permute-start(bf16[3,2,256]{1,2,0:T(8,128)(2,1)} %copy.76), channel_id=1, source_target_pairs={{0,1},{1,2},{2,3},{3,4},{4,5},{5,6},{6,7},{7,8},{8,9},{9,10},{10,1... | collective-permute-start | bytes 9224 | tf_op jit(solution)/shard_map/ppermute | solution.py:13
  10.3 4.0 copy-start.16
  10.3 4.4 copy-start.13
  10.3 3.4 copy-start.30
  77.1 8.7 %copy-start.29 = (f32[3,1,256]{2,1,0:T(1,128)S(1)}, f32[3,1,256]{2,1,0:T(1,128)}, u32[]{:S(2)}) copy-start(f32[3,1,256]{2,1,0:T(1,128)} %get-tuple-element.511) | copy-start | bytes 9220
  77.6 10.8 %copy-start.28 = (f32[16,16]{0,1:T(8,128)S(1)}, f32[16,16]{0,1:T(8,128)}, u32[]{:S(2)}) copy-start(f32[16,16]{0,1:T(8,128)} %get-tuple-element.517) | copy-start | bytes 3076
  100.5 1.6 copy-start
  100.5 2.6 copy-start.6
  100.5 2.7 copy-start.7
  108.1 10.6 %copy-start.1 = (f32[1024,256]{0,1:T(8,128)}, f32[1024,256]{0,1:T(8,128)S(1)}, u32[]{:S(2)}) copy-start(f32[1024,256]{0,1:T(8,128)S(1)} %convert_multiply_fusion.1) | copy-start | bytes 3145732
  109.7 9.3 %copy-start.9 = (f32[16,16,16]{2,1,0:T(8,128)}, f32[16,16,16]{2,1,0:T(8,128)S(1)}, u32[]{:S(2)}) copy-start(f32[16,16,16]{2,1,0:T(8,128)S(1)} %fusion.75) | copy-start | bytes 49156
  112.1 212.9 %all-to-all-start = ((f32[16,1,3,16,256]{4,3,2,1,0:T(8,128)}), f32[16,1,3,16,256]{4,3,2,1,0:T(8,128)}, u32[]{:S(2)}, u32[]{:S(2)}) async-start(f32[16,1,3,16,256]{4,3,2,1,0:T(8,128)} %stack.62), calls=%async_computation | async-start | bytes 1572864 | tf_op jit(solution)/shard_map/all_to_all | solution.py:70
  118.5 1.0 copy-start.8
  264.0 8.1 %copy-start.14 = (f32[16,16]{1,0:T(8,128)S(1)}, f32[16,16]{1,0:T(8,128)}, u32[]{:S(2)}) copy-start(f32[16,16]{1,0:T(8,128)} %get-tuple-element.785) | copy-start | bytes 3076
  264.0 9.0 %copy-start.17 = (f32[16,16]{1,0:T(8,128)S(1)}, f32[16,16]{1,0:T(8,128)}, u32[]{:S(2)}) copy-start(f32[16,16]{1,0:T(8,128)} %get-tuple-element.786) | copy-start | bytes 3076
  274.2 50.8 %copy-start.19 = (f32[16,256]{1,0:T(8,128)S(1)}, f32[16,256]{1,0:T(8,128)}, u32[]{:S(2)}) copy-start(f32[16,256]{1,0:T(8,128)} %neg.32) | copy-start | bytes 49156
  274.2 50.8 %copy-start.32 = (pred[16]{0:T(512)(128)(4,1)S(1)}, pred[16]{0:T(512)(128)(4,1)}, u32[]{:S(2)}) copy-start(pred[16]{0:T(512)(128)(4,1)} %get-tuple-element.531) | copy-start | bytes 52
  274.2 50.8 %copy-start.33 = (pred[16]{0:T(512)(128)(4,1)S(1)}, pred[16]{0:T(512)(128)(4,1)}, u32[]{:S(2)}) copy-start(pred[16]{0:T(512)(128)(4,1)} %get-tuple-element.532) | copy-start | bytes 52
  274.2 50.8 %copy-start.34 = (f32[16]{0:T(128)S(1)}, f32[16]{0:T(128)}, u32[]{:S(2)}) copy-start(f32[16]{0:T(128)} %get-tuple-element.529) | copy-start | bytes 196
  274.3 50.8 %copy-start.35 = (f32[16]{0:T(128)S(1)}, f32[16]{0:T(128)}, u32[]{:S(2)}) copy-start(f32[16]{0:T(128)} %get-tuple-element.530) | copy-start | bytes 196
  274.3 50.8 %copy-start.36 = (f32[16]{0:T(128)S(1)}, f32[16]{0:T(128)}, u32[]{:S(2)}) copy-start(f32[16]{0:T(128)} %maximum_multiply_fusion) | copy-start | bytes 196
  323.4 4.5 copy-start.10
  323.4 4.5 copy-start.27
  323.4 4.6 copy-start.2
  323.4 4.6 copy-start.15
  323.4 4.6 copy-start.31
  323.5 7.0 %copy-start.11 = (f32[16,16]{0,1:T(8,128)S(1)}, f32[16,16]{0,1:T(8,128)}, u32[]{:S(2)}) copy-start(f32[16,16]{0,1:T(8,128)} %get-tuple-element.241) | copy-start | bytes 3076
  323.5 7.0 %copy-start.12 = (f32[16,16]{0,1:T(8,128)S(1)}, f32[16,16]{0,1:T(8,128)}, u32[]{:S(2)}) copy-start(f32[16,16]{0,1:T(8,128)} %get-tuple-element.243) | copy-start | bytes 3076
  323.5 7.0 %copy-start.23 = (f32[16,16]{1,0:T(8,128)S(1)}, f32[16,16]{1,0:T(8,128)}, u32[]{:S(2)}) copy-start(f32[16,16]{1,0:T(8,128)} %get-tuple-element.443) | copy-start | bytes 3076
  323.5 7.0 %copy-start.24 = (f32[16,16]{1,0:T(8,128)S(1)}, f32[16,16]{1,0:T(8,128)}, u32[]{:S(2)}) copy-start(f32[16,16]{1,0:T(8,128)} %get-tuple-element.444) | copy-start | bytes 3076
  323.5 7.0 %copy-start.25 = (f32[16,16]{1,0:T(8,128)S(1)}, f32[16,16]{1,0:T(8,128)}, u32[]{:S(2)}) copy-start(f32[16,16]{1,0:T(8,128)} %param.11) | copy-start | bytes 3076
  323.5 7.0 %copy-start.26 = (f32[16,16]{1,0:T(8,128)S(1)}, f32[16,16]{1,0:T(8,128)}, u32[]{:S(2)}) copy-start(f32[16,16]{1,0:T(8,128)} %param.12) | copy-start | bytes 3076
  325.0 180.5 %copy-start.4 = (f32[16,16,1024]{2,1,0:T(8,128)S(1)}, f32[16,16,1024]{2,1,0:T(8,128)}, u32[]{:S(2)}) copy-start(f32[16,16,1024]{2,1,0:T(8,128)} %rev.29) | copy-start | bytes 3145732
  507.3 2.0 copy-start.5
  507.3 2.0 copy-start.18
  507.3 3.2 copy-start.3
  513.9 12.8 %collective-permute-start.1 = (f32[3,2,256]{1,2,0:T(8,128)}, f32[3,2,256]{1,2,0:T(8,128)}, u32[]{:S(2)}, u32[]{:S(2)}) collective-permute-start(f32[3,2,256]{1,2,0:T(8,128)} %slice.113), channel_id=1, source_target_pairs={{1,0},{2,1},{3,2},{4,3},{5,4},{6,5},{7,6},{8,7},{9,8},{10,9},{11,1... | collective-permute-start | bytes 18440 | tf_op jit(solution)/shard_map/ppermute | solution.py:13
  517.8 10.1 %copy-start.20 = (f32[3,256]{1,0:T(4,128)S(1)}, f32[3,256]{1,0:T(4,128)}, u32[]{:S(2)}) copy-start(f32[3,256]{1,0:T(4,128)} %get-tuple-element.527) | copy-start | bytes 9220
  517.8 10.1 %copy-start.21 = (f32[3,256]{1,0:T(4,128)S(1)}, f32[3,256]{1,0:T(4,128)}, u32[]{:S(2)}) copy-start(f32[3,256]{1,0:T(4,128)} %get-tuple-element.528) | copy-start | bytes 9220
  517.8 10.1 %copy-start.22 = (f32[3,1,256]{2,0,1:T(4,128)S(1)}, f32[3,1,256]{2,0,1:T(4,128)}, u32[]{:S(2)}) copy-start(f32[3,1,256]{2,0,1:T(4,128)} %copy.132) | copy-start | bytes 9220
